TPU v7x, 32 devices: a whole 2x2x4 slice. The times are simulated.
32 devices in a mesh: dp: 16 (over z, y, x), grp: 2 (over core).
Axes of the slice: x: 2, y: 2, z: 4, core: 2. Of those that a mesh axis runs over, the one named last changes fastest.
Arguments:
- query_features: bfloat16 [32768, 512], P(('dp', 'grp')), may hold values from -256 to 256
- query_weights: bfloat16 [32768], P(('dp', 'grp')), may hold values from 0.5 to 13.5, as said below
- positive_index: int32 [32768], P(('dp', 'grp')), may hold values from 0 to 511
- item_features: bfloat16 [512, 512], P(('dp', 'grp')), may hold values from -6 to 6
- item_ids: int32 [512], P(('dp', 'grp')), may hold values from 0 to 255
- item_logq: bfloat16 [512], P(('dp', 'grp')), may hold values from -14 to -11
- query_w_in: bfloat16 [512, 1024], replicated, may hold values from -0.25 to 0.25
- query_w_out: bfloat16 [1024, 256], replicated, may hold values from -0.1875 to 0.1875
- item_w_in: bfloat16 [512, 1024], replicated, may hold values from -0.25 to 0.25
- item_w_out: bfloat16 [1024, 256], replicated, may hold values from -0.1875 to 0.1875
Outputs:
- grad_query_w_in: float32 [512, 1024], replicated
- grad_query_w_out: float32 [1024, 256], replicated
- grad_item_w_in: float32 [512, 1024], replicated
- grad_item_w_out: float32 [1024, 256], replicated
Inputs may be any that keep to these rules, and one draw needn't show every extreme that they name: `query_weights`: positive weights. `item_ids`: an id may occur several times in the sample set.
All inputs are finite; a program needn't handle non-finite values.
Results may differ from a plain program's by a relative error of at most 0.013.
Values may be sent and summed in bfloat16 or wider, within the bound.
A program may use at most 128 MiB of HBM per device.

v0:
```python
import jax
import jax.numpy as jnp
from jax import lax
from jax.sharding import PartitionSpec as P

score_scale = 0.25
loss_scale = 1024.0


def silu_slope(values):
    gate = jax.nn.sigmoid(values)
    return gate * (1.0 + values * (1.0 - gate))


def tower(features, weight_in, weight_out):
    pre_act = jnp.dot(features, weight_in, preferred_element_type=jnp.float32)
    hidden = jax.nn.silu(pre_act).astype(jnp.bfloat16)
    embedding = jnp.dot(hidden, weight_out, preferred_element_type=jnp.float32).astype(jnp.bfloat16)
    return (pre_act, hidden, embedding)


def tower_back(features, pre_act, hidden, weight_out, embed_grad):
    grad_out = jnp.dot(hidden.T, embed_grad, preferred_element_type=jnp.float32)
    hidden_grad = jnp.dot(embed_grad, weight_out.T, preferred_element_type=jnp.float32)
    pre_grad = (hidden_grad * silu_slope(pre_act)).astype(jnp.bfloat16)
    grad_in = jnp.dot(features.T, pre_grad, preferred_element_type=jnp.float32)
    return (grad_in, grad_out)


def item_scores(query_rows, items, item_bias, item_codes, columns, positives, pos_codes):
    raw_scores = lax.dot_general(
        query_rows, items, (((1,), (1,)), ((), ())), preferred_element_type=jnp.float32
    )
    scores = score_scale * raw_scores - item_bias.astype(jnp.float32)[None, :]
    masked_hits = (item_codes[None, :] == pos_codes[:, None]) & (
        columns[None, :] != positives[:, None]
    )
    return jnp.where(masked_hits, -jnp.inf, scores)


def partial_stats(scores):
    row_max = jnp.maximum(jnp.max(scores, axis=1), -1e30)
    row_sum = jnp.sum(jnp.exp(scores - row_max[:, None]), axis=1)
    return (row_max, row_sum)


def finish(scores, row_max, row_sum, columns, positives, weights):
    probability = jnp.exp(scores - row_max[:, None]) / row_sum[:, None]
    target = (columns[None, :] == positives[:, None]).astype(jnp.float32)
    return (weights.astype(jnp.float32)[:, None] * (probability - target)).astype(jnp.bfloat16)


def positive_codes(every_code, positives):
    slots = jnp.arange(every_code.shape[0], dtype=jnp.int32)
    return jnp.sum(jnp.where(positives[:, None] == slots[None, :], every_code[None, :], 0), axis=1)


def on_device(
    query_features,
    query_weights,
    positive_index,
    item_features,
    item_ids,
    item_logq,
    query_w_in,
    query_w_out,
    item_w_in,
    item_w_out,
):
    weight_part = jnp.sum(query_weights.astype(jnp.float32))
    weight_total = lax.psum(weight_part, ("dp", "grp"))
    query_pre, query_hidden, query_embed = tower(query_features, query_w_in, query_w_out)
    item_pre, item_hidden, item_embed = tower(item_features, item_w_in, item_w_out)
    items_all, bias_all, codes_all = (
        lax.all_gather(item_embed, ("dp", "grp"), axis=0, tiled=True),
        lax.all_gather(item_logq, ("dp", "grp"), axis=0, tiled=True),
        lax.all_gather(item_ids, ("dp", "grp"), axis=0, tiled=True),
    )
    columns = jnp.arange(items_all.shape[0], dtype=jnp.int32)
    pos_codes = positive_codes(codes_all, positive_index)
    scores = item_scores(
        query_embed, items_all, bias_all, codes_all, columns, positive_index, pos_codes
    )
    row_max, row_sum = partial_stats(scores)
    dlogit = finish(scores, row_max, row_sum, columns, positive_index, query_weights)
    query_grad = (
        score_scale * jnp.dot(dlogit, items_all, preferred_element_type=jnp.float32)
    ).astype(jnp.bfloat16)
    item_grad = lax.psum_scatter(
        score_scale
        * lax.dot_general(
            dlogit, query_embed, (((0,), (0,)), ((), ())), preferred_element_type=jnp.float32
        ),
        ("dp", "grp"),
        scatter_dimension=0,
        tiled=True,
    ).astype(jnp.bfloat16)
    query_in_part, query_out_part = tower_back(
        query_features, query_pre, query_hidden, query_w_out, query_grad
    )
    item_in_part, item_out_part = tower_back(
        item_features, item_pre, item_hidden, item_w_out, item_grad
    )
    query_in_sum, query_out_sum, item_in_sum, item_out_sum = lax.psum(
        (query_in_part, query_out_part, item_in_part, item_out_part), ("dp", "grp")
    )
    factor = loss_scale / weight_total
    return (
        query_in_sum * factor,
        query_out_sum * factor,
        item_in_sum * factor,
        item_out_sum * factor,
    )


def solution(mesh):
    in_specs = (
        P(("dp", "grp"), None),
        P(("dp", "grp")),
        P(("dp", "grp")),
        P(("dp", "grp"), None),
        P(("dp", "grp")),
        P(("dp", "grp")),
        P(),
        P(),
        P(),
        P(),
    )
    out_specs = (P(), P(), P(), P())
    return jax.shard_map(
        on_device, mesh=mesh, in_specs=in_specs, out_specs=out_specs, check_vma=False
    )
```

profile of v0, /device:TPU:0, one launch (start us, length us, event | category | flops | bytes accessed | tf_op | source)
XLA Modules:
  0.0 457.4 jit_solution(10545431475410207212)
XLA Ops:
  7.2 0.0 reduce-scatter.2.cloned.1.call-start
  7.2 1.6 fusion.16
  8.8 1.2 convolution_convert_fusion.1
  10.0 43.9 %all_gather.10 = bf16[512,256]{1,0:T(8,128)(2,1)S(1)} all-gather(bf16[16,256]{1,0:T(8,128)(2,1)S(1)} %convolution_convert_fusion.1), channel_id=1, replica_groups=mesh['dp'=16,'grp'=2] {'dp','grp'}, dimensions={0}, use_global_device_ids=true | all-gather | bytes 270336 | tf_op jit(solution)/shard_map/all_gather | solution.py:75
  54.0 0.8 dynamic-update-slice
  54.8 36.8 %all-reduce = s32[512]{0:T(512)S(1)} all-reduce(s32[512]{0:T(512)S(1)} %dynamic-update-slice), channel_id=1, replica_groups=mesh['dp'=16,'grp'=2] {'dp','grp'}, use_global_device_ids=true, to_apply=%add | all-reduce | flops 512 | bytes 4096
  91.6 0.8 dynamic-update-slice.1
  92.5 41.1 %all-reduce.1 = bf16[512]{0:T(512)(128)(2,1)S(1)} all-reduce(bf16[512]{0:T(512)(128)(2,1)S(1)} %dynamic-update-slice.1), channel_id=1, replica_groups=mesh['dp'=16,'grp'=2] {'dp','grp'}, use_global_device_ids=true, to_apply=%add.1 | all-reduce | flops 512 | bytes 2048
  133.6 4.8 %multiply_convert_fusion.1 = (bf16[1024,1024]{1,0:T(8,128)(2,1)S(1)}, f32[1024,1024]{1,0:T(8,128)}) fusion(bf16[1024,512]{1,0:T(8,128)(2,1)S(1)} %copy-done, bf16[512,1024]{1,0:T(8,128)(2,1)} %param.16), kind=kOutput, calls=%fused_computation.1 | convolution fusion | flops 1078984704 | bytes 8388608 | tf_op jit(solution)/shard_map/dot_general | solution.py:16
  138.4 0.7 convolution_convert_fusion
  139.1 0.6 copy-done.7
  139.7 0.3 select_reduce_fusion
  140.0 0.8 fusion.15
  140.8 0.3 fusion.1
  141.2 0.7 multiply_convert_fusion.2
  141.8 1.2 convolution_multiply_fusion.1
  143.1 0.0 all-reduce.5.cloned.1.call-start
  143.2 0.5 fusion.2
  143.7 1.1 copy-done.8
  144.7 1.7 fusion.17
  146.5 6.1 %convolution_bitcast_fusion.1 = f32[512,1024]{0,1:T(8,128)} fusion(bf16[1024,512]{1,0:T(8,128)(2,1)S(1)} %copy-done, f32[1024,1024]{1,0:T(8,128)} %get-tuple-element.13, bf16[1024,256]{1,0:T(8,128)(2,1)S(1)} %fusion.2, bf16[1024,256]{1,0:T(8,128)(2,1)S(1)} %copy-done.6), kind=kOutput, calls=%fused_computation.13 | convolution fusion | flops 1620049920 | bytes 8388608 | tf_op jit(solution)/shard_map/dot_general | solution.py:26
  152.5 126.6 %reduce-scatter.2.cloned.1.call-done = f32[16,256]{1,0:T(8,128)} async-done(((f32[512,256]{1,0:T(8,128)}), f32[16,256]{1,0:T(8,128)}) %reduce-scatter.2.cloned.1.call-update) | async-done | bytes 16400 | tf_op jit(solution)/shard_map/reduce_scatter | solution.py:89
  279.2 2.7 convolution_bitcast_fusion
  281.9 1.3 fusion.9
  283.3 0.0 all-reduce.5.cloned.1.call-update
  283.3 0.6 convert_reduce_fusion
  283.9 38.4 %psum.36 = f32[]{:T(128)} all-reduce(f32[]{:T(128)} %convert_reduce_fusion), channel_id=1, replica_groups=mesh['dp'=16,'grp'=2] {'dp','grp'}, use_global_device_ids=true, to_apply=%region_5.6 | all-reduce | flops 1 | bytes 8 | tf_op jit(solution)/shard_map/psum | solution.py:71
  322.9 115.9 %all-reduce.5.cloned.1.call-done = (f32[512,1024]{0,1:T(8,128)}, f32[1024,256]{1,0:T(8,128)}, f32[512,1024]{0,1:T(8,128)}, f32[1024,256]{1,0:T(8,128)}) async-done(((f32[512,1024]{0,1:T(8,128)}, f32[1024,256]{1,0:T(8,128)}, f32[512,1024]{0,1:T(8,128)}, f32[1024,256]{1,0:T(8,128)}), (f32[512,1024]{0,1:T(8,128)}, f32[1024,256]{1,0:T(8,128)}, f32[512,1024]{0,1:T(8,128)}, ...) | async-done | bytes 6291472 | tf_op jit(solution)/shard_map/psum | solution.py:104
  438.8 4.0 broadcast_multiply_fusion
  442.9 2.9 copy.14
  445.8 1.8 copy.15
  447.6 3.0 broadcast_multiply_fusion.2
  (22 shorter events, 0.1 us)
Async XLA Ops:
  7.2 126.5 %copy-start = (bf16[1024,512]{1,0:T(8,128)(2,1)S(1)}, bf16[1024,512]{1,0:T(8,128)(2,1)}, u32[]{:S(2)}) copy-start(bf16[1024,512]{1,0:T(8,128)(2,1)} %param.10) | copy-start | bytes 3145732
  7.2 272.0 %reduce-scatter.2.cloned.1.call-start = ((), (), s32[]{:S(2)}) async-start(), calls=%async_computation.1 | async-start | bytes 540672 | tf_op jit(solution)/shard_map/reduce_scatter | solution.py:89
  133.6 4.8 %copy-start.6 = (bf16[1024,256]{1,0:T(8,128)(2,1)S(1)}, bf16[1024,256]{1,0:T(8,128)(2,1)}, u32[]{:S(2)}) copy-start(bf16[1024,256]{1,0:T(8,128)(2,1)} %param.17) | copy-start | bytes 1572868
  138.4 1.3 copy-start.7
  138.4 1.3 copy-start.4
  140.0 0.8 copy-start.5
  143.1 295.7 %all-reduce.5.cloned.1.call-start = ((), (), s32[]{:S(2)}) async-start(), calls=%async_computation.2 | async-start | bytes 12582912 | tf_op jit(solution)/shard_map/psum | solution.py:104
  143.2 1.6 copy-start.8
  146.5 132.7 %copy-start.1 = (bf16[1024,256]{1,0:T(8,128)(2,1)S(1)}, bf16[1024,256]{1,0:T(8,128)(2,1)}, u32[]{:S(2)}) copy-start(bf16[1024,256]{1,0:T(8,128)(2,1)} %param.19) | copy-start | bytes 1572868
  146.5 132.7 %copy-start.2 = (bf16[16,512]{1,0:T(8,128)(2,1)S(1)}, bf16[16,512]{1,0:T(8,128)(2,1)}, u32[]{:S(2)}) copy-start(bf16[16,512]{1,0:T(8,128)(2,1)} %param.13) | copy-start | bytes 49156
  279.2 2.8 copy-start.3
Sparse Core Ops, SparseCore 0:
  143.2 135.9 reduce-scatter.1
  285.8 153.0 all-reduce.4
where the time goes:
time: 458 us; the launch traced here: 457 us
  waiting for transfers between devices  243 us (53%)
  blocking collectives  160 us (35%)
  matrix products  22.6 us (5%)
  between operations  14.8 us (3%)
  other arithmetic  8.95 us (2%)
  local copies, waits for them, and re-layouts  8.09 us (2%)
    reduce_scatter x1, waiting for transfers between devices, on_device(): lax.psum_scatter(score_scale * lax.dot_general(dlogit, query_embed, (((0,...  127 us
    psum x1, waiting for transfers between devices, on_device(): lax.psum((query_in_part, query_out_part, item_in_part, item_out_part), ('...  116 us
    unnamed x2, blocking collectives  78 us
    all_gather x1, blocking collectives, on_device(): lax.all_gather(item_embed, ('dp', 'grp'), axis=0, tiled=True)  43.9 us
    psum x1, blocking collectives, on_device(): weight_total = lax.psum(weight_part, ('dp', 'grp'))  38.4 us
  transfers between devices with their start and end apart: 2, of which 2 were waited for; matrix products, arithmetic and copies ran while one was open for 2% of the time, Pallas kernels for 0%

commit v1 on v0

--- a/solution.py
+++ b/solution.py
@@ -5,6 +5,14 @@
 
 score_scale = 0.25
 loss_scale = 1024.0
+
+
+def gather_from_all(array, axis, dim):
+    size = lax.axis_size(axis)
+    repeats = [size if d == dim else 1 for d in range(array.ndim)]
+    return lax.all_to_all(
+        jnp.tile(array, repeats), axis, split_axis=dim, concat_axis=dim, tiled=True
+    )
 
 
 def silu_slope(values):
@@ -72,7 +80,7 @@
     query_pre, query_hidden, query_embed = tower(query_features, query_w_in, query_w_out)
     item_pre, item_hidden, item_embed = tower(item_features, item_w_in, item_w_out)
     items_all, bias_all, codes_all = (
-        lax.all_gather(item_embed, ("dp", "grp"), axis=0, tiled=True),
+        gather_from_all(item_embed, ("dp", "grp"), 0),
         lax.all_gather(item_logq, ("dp", "grp"), axis=0, tiled=True),
         lax.all_gather(item_ids, ("dp", "grp"), axis=0, tiled=True),
     )

time: 458 us -> 425 us (0.928)
  blocking collectives: 160 us -> 119 us
  starting transfers between devices: 0.08 us -> 7.41 us
    all_gather x1 -> x0, blocking collectives: 43.9 us -> none  [on_device(): lax.all_gather(item_embed, ('dp', 'grp'), axis=0, tiled=True)]
    all_to_all x0 -> x1, starting transfers between devices: none -> 7.33 us  [gather_from_all(): lax.all_to_all(jnp.tile(array, repeats), axis, split_axis=dim, concat_axi...]
  transfers between devices with their start and end apart: 2 -> 3, of which waited for: 2 -> 2; matrix products, arithmetic and copies ran while one was open for 2% -> 4% of each run, Pallas kernels for 0% -> 0%
where the time goes in v1:
time: 425 us
  waiting for transfers between devices  243 us (57%)
  blocking collectives  119 us (28%)
  matrix products  25.3 us (6%)
  between operations  14.8 us (3%)
  other arithmetic  8.95 us (2%)
  starting transfers between devices  7.41 us (2%)
  local copies, waits for them, and re-layouts  5.93 us (1%)
    reduce_scatter x1, waiting for transfers between devices, on_device(): lax.psum_scatter(score_scale * lax.dot_general(dlogit, query_embed, (((0,...  127 us
    psum x1, waiting for transfers between devices, on_device(): lax.psum((query_in_part, query_out_part, item_in_part, item_out_part), ('...  116 us
    unnamed x2, blocking collectives  80.5 us
    psum x1, blocking collectives, on_device(): weight_total = lax.psum(weight_part, ('dp', 'grp'))  38.4 us
    dot_general x2, matrix products, tower_back(): grad_in = jnp.dot(features.T, pre_grad, preferred_element_type=jnp.float32)  8.77 us
  transfers between devices with their start and end apart: 3, of which 2 were waited for; matrix products, arithmetic and copies ran while one was open for 4% of the time, Pallas kernels for 0%

profile of v1, /device:TPU:0, one launch (start us, length us, event | category | flops | bytes accessed | tf_op | source)
XLA Modules:
  0.0 424.7 jit_solution(18428963756166516648)
XLA Ops:
  7.2 1.6 fusion.16
  8.8 1.2 convolution_convert_fusion.1
  10.1 0.7 tile.2
  10.8 7.3 %all-to-all-start = ((bf16[32,16,256]{2,1,0:T(8,128)(2,1)}), bf16[32,16,256]{2,1,0:T(8,128)(2,1)S(1)}, u32[]{:S(2)}, u32[]{:S(2)}) async-start(bf16[32,16,256]{2,1,0:T(8,128)(2,1)} %tile.2), calls=%async_computation | async-start | bytes 524288 | tf_op jit(solution)/shard_map/all_to_all | solution.py:13
  18.2 0.0 reduce-scatter.2.cloned.1.call-start
  18.2 4.3 %multiply_convert_fusion.1 = (bf16[1024,1024]{1,0:T(8,128)(2,1)}, f32[1024,1024]{1,0:T(8,128)}) fusion(bf16[1024,512]{1,0:T(8,128)(2,1)S(1)} %copy-done, bf16[512,1024]{1,0:T(8,128)(2,1)S(1)} %copy-done.6), kind=kOutput, calls=%fused_computation.1 | convolution fusion | flops 1078984704 | bytes 8388608 | tf_op jit(solution)/shard_map/dot_general | solution.py:24
  22.5 0.2 dynamic-update-slice.1
  22.7 40.5 %all-reduce.1 = bf16[512]{0:T(512)(128)(2,1)S(1)} all-reduce(bf16[512]{0:T(512)(128)(2,1)S(1)} %dynamic-update-slice.1), channel_id=1, replica_groups=mesh['dp'=16,'grp'=2] {'dp','grp'}, use_global_device_ids=true, to_apply=%add.1 | all-reduce | flops 512 | bytes 2048
  63.3 0.2 dynamic-update-slice
  63.5 40.0 %all-reduce = s32[512]{0:T(512)S(1)} all-reduce(s32[512]{0:T(512)S(1)} %dynamic-update-slice), channel_id=1, replica_groups=mesh['dp'=16,'grp'=2] {'dp','grp'}, use_global_device_ids=true, to_apply=%add | all-reduce | flops 512 | bytes 4096
  103.5 0.3 select_reduce_fusion
  103.9 2.3 convolution_convert_fusion
  106.2 0.8 fusion.15
  107.0 0.3 fusion.1
  107.3 0.7 multiply_convert_fusion.2
  108.0 1.2 convolution_multiply_fusion.1
  109.2 0.5 fusion.2
  109.7 0.0 reduce-scatter.2.cloned.1.call-update
  109.7 0.0 all-reduce.5.cloned.1.call-start
  109.8 3.3 fusion.17
  113.1 6.0 %convolution_bitcast_fusion.1 = f32[512,1024]{0,1:T(8,128)} fusion(bf16[1024,512]{1,0:T(8,128)(2,1)S(1)} %copy-done, f32[1024,1024]{1,0:T(8,128)} %get-tuple-element.13, bf16[1024,256]{1,0:T(8,128)(2,1)S(1)} %fusion.2, bf16[1024,256]{1,0:T(8,128)(2,1)S(1)} %copy-done.7), kind=kOutput, calls=%fused_computation.13 | convolution fusion | flops 1620049920 | bytes 8388608 | tf_op jit(solution)/shard_map/dot_general | solution.py:34
  119.1 127.2 %reduce-scatter.2.cloned.1.call-done = f32[16,256]{1,0:T(8,128)} async-done(((f32[512,256]{1,0:T(8,128)}), f32[16,256]{1,0:T(8,128)}) %reduce-scatter.2.cloned.1.call-update) | async-done | bytes 16400 | tf_op jit(solution)/shard_map/reduce_scatter | solution.py:97
  246.3 2.7 convolution_bitcast_fusion
  249.1 1.3 fusion.9
  250.4 0.0 all-reduce.5.cloned.1.call-update
  250.4 0.6 convert_reduce_fusion
  251.0 38.4 %psum.36 = f32[]{:T(128)} all-reduce(f32[]{:T(128)} %convert_reduce_fusion), channel_id=1, replica_groups=mesh['dp'=16,'grp'=2] {'dp','grp'}, use_global_device_ids=true, to_apply=%region_5.6 | all-reduce | flops 1 | bytes 8 | tf_op jit(solution)/shard_map/psum | solution.py:79
  290.0 116.1 %all-reduce.5.cloned.1.call-done = (f32[512,1024]{0,1:T(8,128)}, f32[1024,256]{1,0:T(8,128)}, f32[512,1024]{0,1:T(8,128)}, f32[1024,256]{1,0:T(8,128)}) async-done(((f32[512,1024]{0,1:T(8,128)}, f32[1024,256]{1,0:T(8,128)}, f32[512,1024]{0,1:T(8,128)}, f32[1024,256]{1,0:T(8,128)}), (f32[512,1024]{0,1:T(8,128)}, f32[1024,256]{1,0:T(8,128)}, f32[512,1024]{0,1:T(8,128)}, ...) | async-done | bytes 6291472 | tf_op jit(solution)/shard_map/psum | solution.py:112
  406.1 4.0 broadcast_multiply_fusion
  410.1 2.9 copy.14
  413.0 1.8 copy.15
  414.8 3.0 broadcast_multiply_fusion.2
  (26 shorter events, 0.1 us)
Async XLA Ops:
  7.2 11.1 %copy-start = (bf16[1024,512]{1,0:T(8,128)(2,1)S(1)}, bf16[1024,512]{1,0:T(8,128)(2,1)}, u32[]{:S(2)}) copy-start(bf16[1024,512]{1,0:T(8,128)(2,1)} %param.10) | copy-start | bytes 3145732
  7.2 11.1 %copy-start.6 = (bf16[512,1024]{1,0:T(8,128)(2,1)S(1)}, bf16[512,1024]{1,0:T(8,128)(2,1)}, u32[]{:S(2)}) copy-start(bf16[512,1024]{1,0:T(8,128)(2,1)} %param.16) | copy-start | bytes 3145732
  10.8 95.4 %all-to-all-start = ((bf16[32,16,256]{2,1,0:T(8,128)(2,1)}), bf16[32,16,256]{2,1,0:T(8,128)(2,1)S(1)}, u32[]{:S(2)}, u32[]{:S(2)}) async-start(bf16[32,16,256]{2,1,0:T(8,128)(2,1)} %tile.2), calls=%async_computation | async-start | bytes 524288 | tf_op jit(solution)/shard_map/all_to_all | solution.py:13
  18.1 4.4 %copy-start.8 = (bf16[16]{0:T(256)(128)(2,1)S(1)}, bf16[16]{0:T(256)(128)(2,1)}, u32[]{:S(2)}) copy-start(bf16[16]{0:T(256)(128)(2,1)} %param.15) | copy-start | bytes 100
  18.1 45.1 %copy-start.5 = (bf16[1024]{0:T(1024)(128)(2,1)S(1)}, bf16[1024]{0:T(1024)(128)(2,1)}, u32[]{:S(2)}) copy-start(bf16[1024]{0:T(1024)(128)(2,1)} %param.11) | copy-start | bytes 6148
  18.1 45.1 %copy-start.9 = (s32[16]{0:T(128)S(1)}, s32[16]{0:T(128)}, u32[]{:S(2)}) copy-start(s32[16]{0:T(128)} %param.14) | copy-start | bytes 196
  18.2 85.4 %copy-start.4 = (s32[1024]{0:T(1024)S(1)}, s32[1024]{0:T(1024)}, u32[]{:S(2)}) copy-start(s32[1024]{0:T(1024)} %param.12) | copy-start | bytes 12292
  18.2 85.7 %copy-start.7 = (bf16[1024,256]{1,0:T(8,128)(2,1)S(1)}, bf16[1024,256]{1,0:T(8,128)(2,1)}, u32[]{:S(2)}) copy-start(bf16[1024,256]{1,0:T(8,128)(2,1)} %param.17) | copy-start | bytes 1572868
  18.2 228.1 %reduce-scatter.2.cloned.1.call-start = ((), (), s32[]{:S(2)}) async-start(), calls=%async_computation.2 | async-start | bytes 540672 | tf_op jit(solution)/shard_map/reduce_scatter | solution.py:97
  109.7 296.4 %all-reduce.5.cloned.1.call-start = ((), (), s32[]{:S(2)}) async-start(), calls=%async_computation.3 | async-start | bytes 12582912 | tf_op jit(solution)/shard_map/psum | solution.py:112
  113.1 133.2 %copy-start.1 = (bf16[1024,256]{1,0:T(8,128)(2,1)S(1)}, bf16[1024,256]{1,0:T(8,128)(2,1)}, u32[]{:S(2)}) copy-start(bf16[1024,256]{1,0:T(8,128)(2,1)} %param.19) | copy-start | bytes 1572868
  113.1 133.2 %copy-start.2 = (bf16[16,512]{1,0:T(8,128)(2,1)S(1)}, bf16[16,512]{1,0:T(8,128)(2,1)}, u32[]{:S(2)}) copy-start(bf16[16,512]{1,0:T(8,128)(2,1)} %param.13) | copy-start | bytes 49156
  246.3 2.8 copy-start.3
Sparse Core Ops, SparseCore 0:
  109.8 136.4 reduce-scatter.1
  252.9 153.1 all-reduce.4
